TPU v7x, 32 devices: a whole 2x2x4 slice. The times are simulated.
32 devices in a mesh: ep: 16 (over z, x, core), tp: 2 (over y).
Axes of the slice: x: 2, y: 2, z: 4, core: 2. Of those that a mesh axis runs over, the one named last changes fastest.
Arguments:
- attn: bfloat16 [2048, 2048], P('ep', 'tp'), may hold values from -6 to 6
- o_weight: bfloat16 [2048, 2048], P('tp'), may hold values from -0.125 to 0.125
- residual: bfloat16 [2048, 2048], P(('ep', 'tp')), may hold values from -6 to 6
- norm_gain: float32 [2048], replicated, may hold values from 0.5 to 2
- routes: int32 [2048, 6], P('ep'), may hold values from 0 to 15, all different within a row; in each aligned block of 64 rows (0 to 63, 64 to 127, ...) at most 32 rows name the same one
- route_logits: float32 [2048, 6], P('ep'), may hold values from -6 to 6
- expert_in: bfloat16 [16, 2, 2048, 1408], P('ep', None, None, 'tp'), may hold values from -0.125 to 0.125
- expert_out: bfloat16 [16, 2048, 1408], P('ep', None, 'tp'), may hold values from -0.15625 to 0.15625
- shared_in: bfloat16 [2, 2048, 1408], P(None, None, 'tp'), may hold values from -0.125 to 0.125
- shared_out: bfloat16 [2048, 1408], P(None, 'tp'), may hold values from -0.15625 to 0.15625
Outputs:
- block_out: bfloat16 [2048, 2048], P(('ep', 'tp'))
Inputs may be any that keep to these rules, and one draw needn't show every extreme that they name: `routes`: each row names 6 different experts. Within each aligned block of 64 rows (the rows of one device) no expert is named by more than 32 rows, a bound that some block reaches.
All inputs are finite; a program needn't handle non-finite values.
Results may differ from a plain program's by a relative error of at most 0.0058.
Values may be sent and summed in bfloat16 or wider, within the bound.
A program may use at most 192 MiB of HBM per device.

v0:
```python
import jax
import jax.numpy as jnp
from jax import lax
from jax.experimental import pallas as pl
from jax.experimental.pallas import tpu as pltpu
from jax.sharding import PartitionSpec as P

PIECES = 4
GATHER_STEPS = (0, 2, 5, 8)


def slot_places(route_rows, capacity, experts):
    flat_routes = route_rows.reshape(-1)
    onehot = (flat_routes[:, None] == jnp.arange(experts, dtype=jnp.int32)[None, :]).astype(
        jnp.int32
    )
    before = jnp.cumsum(onehot, axis=0) - onehot
    ranks = jnp.sum(before * onehot, axis=1)
    return flat_routes * capacity + ranks


def fill_slots(source_rows, places, capacity, experts, topk):
    copies = jnp.repeat(source_rows, topk, axis=0)
    empty_slots = jnp.zeros((experts * capacity, source_rows.shape[1]), source_rows.dtype)
    return empty_slots.at[places].set(copies)


def route_weights(logits):
    sigmoids = jax.nn.sigmoid(logits)
    return 2.446 * sigmoids / jnp.sum(sigmoids, axis=-1, keepdims=True)


def expert_part(slots, w_in, w_out):
    gate_val = jnp.einsum("slcd,ldf->slcf", slots, w_in[:, 0], preferred_element_type=jnp.float32)
    up_val = jnp.einsum("slcd,ldf->slcf", slots, w_in[:, 1], preferred_element_type=jnp.float32)
    active = (jax.nn.silu(gate_val) * up_val).astype(jnp.bfloat16)
    return jnp.einsum("slcf,ldf->slcd", active, w_out, preferred_element_type=jnp.float32)


def shared_part(source_rows, s_in, s_out):
    gate_val = jnp.dot(source_rows, s_in[0], preferred_element_type=jnp.float32)
    up_val = jnp.dot(source_rows, s_in[1], preferred_element_type=jnp.float32)
    active = (jax.nn.silu(gate_val) * up_val).astype(jnp.bfloat16)
    return jnp.einsum("tf,df->td", active, s_out, preferred_element_type=jnp.float32)


def combine_slots(values, places, weights, topk):
    picked = values[places].reshape(-1, topk, values.shape[1])
    return jnp.sum(picked * weights[:, :, None], axis=1)


def slotted_shards(
    attn,
    o_weight,
    residual,
    norm_gain,
    routes,
    route_logits,
    expert_in,
    expert_out,
    shared_in,
    shared_out,
):
    tok_rows = residual.shape[0]
    width = residual.shape[1]
    topk = routes.shape[1]
    tp_count = lax.axis_size("tp")
    ep_count = lax.axis_size("ep")
    local_experts = expert_in.shape[0]
    experts = local_experts * ep_count
    capacity = max(2, (4 * tok_rows * topk + 3 * experts - 1) // (3 * experts))
    attn_out = lax.psum_scatter(
        jnp.dot(attn, o_weight, preferred_element_type=jnp.float32),
        "tp",
        scatter_dimension=0,
        tiled=True,
    )
    hidden = residual.astype(jnp.float32) + attn_out
    inv_norm = lax.rsqrt(jnp.mean(hidden * hidden, axis=-1, keepdims=True) + 1e-06)
    normed = (hidden * inv_norm * norm_gain).astype(jnp.bfloat16)
    group_rows = lax.all_gather(normed, "tp", axis=0, tiled=True)
    group_cap = tp_count * capacity
    places = slot_places(routes, group_cap, experts)
    outgoing = fill_slots(group_rows, places, group_cap, experts, topk)
    incoming = lax.all_to_all(outgoing, "ep", split_axis=0, concat_axis=0, tiled=True)
    partial_value = expert_part(
        incoming.reshape(ep_count, local_experts, group_cap, width), expert_in, expert_out
    )
    returned = lax.all_to_all(
        partial_value.reshape(-1, width), "ep", split_axis=0, concat_axis=0, tiled=True
    )
    mixture = combine_slots(returned, places, route_weights(route_logits), topk)
    mixture = mixture + shared_part(group_rows, shared_in, shared_out)
    moe_sum = lax.psum_scatter(mixture, "tp", scatter_dimension=0, tiled=True)
    return (hidden + moe_sum).astype(jnp.bfloat16)


def place():
    ep = lax.axis_index("ep")
    return lax.div(ep, 4), lax.rem(lax.div(ep, 2), 2), lax.rem(ep, 2), lax.axis_index("tp")


def device_at(z, x, core, y):
    return (z * 4 + x * 2 + core, y)


def peers(z, x, core, y):
    along_z = [device_at(lax.rem(z + step, 4), x, core, y) for step in (1, 2, 3)]
    return (
        along_z,
        device_at(z, 1 - x, core, y),
        device_at(z, x, 1 - core, y),
        device_at(z, x, core, 1 - y),
    )


def greet(along_z, x_peer, core_peer, y_peer):
    barrier = pltpu.get_barrier_semaphore()
    for peer in (*along_z, x_peer, core_peer, y_peer):
        pl.semaphore_signal(
            barrier, inc=1, device_id=peer, device_id_type=pl.DeviceIdType.MESH
        )
    pl.semaphore_wait(barrier, 6)


def remote(src, dst, send_sem, recv_sem, peer):
    copy = pltpu.make_async_remote_copy(
        src_ref=src,
        dst_ref=dst,
        send_sem=send_sem,
        recv_sem=recv_sem,
        device_id=peer,
        device_id_type=pl.DeviceIdType.MESH,
    )
    copy.start()
    return copy


def gather_kernel(
    in_ref, w_ref, out_ref, w_out, own_sem, z_send, z_recv, send, recv, w_send, w_recv
):
    z, x, core, y = place()
    along_z, x_peer, core_peer, y_peer = peers(z, x, core, y)
    ep = lax.axis_index("ep")
    rows = in_ref.shape[0] // PIECES
    own = pltpu.make_async_copy(in_ref, out_ref.at[z, x, core, y], own_sem)
    own.start()
    others = [lax.rem(ep + step, 16) for step in range(1, 16)]
    barrier = pltpu.get_barrier_semaphore()
    for peer in [(other, y) for other in others] + [y_peer]:
        pl.semaphore_signal(
            barrier, inc=1, device_id=peer, device_id_type=pl.DeviceIdType.MESH
        )
    pl.semaphore_wait(barrier, 16)
    started = []
    z_copies = []
    for q in range(PIECES):
        piece = pl.ds(q * rows, rows)
        z_copies.append(
            [
                remote(
                    in_ref.at[piece],
                    out_ref.at[z, x, core, y, piece],
                    z_send.at[q, i],
                    z_recv.at[q, i],
                    along_z[i],
                )
                for i in range(3)
            ]
        )
        started.extend(z_copies[q])
    w_copies = [
        remote(w_ref.at[other], w_out.at[ep], w_send.at[i], w_recv.at[i], (other, y))
        for i, other in enumerate(others)
    ]
    w_out[ep] = w_ref[ep]
    own.wait()
    waiting = [None] * PIECES
    order = sorted(
        ((stage, q) for stage in range(4) for q in range(PIECES)),
        key=lambda item: (item[1] + GATHER_STEPS[item[0]], item[0]),
    )
    for stage, q in order:
        piece = pl.ds(q * rows, rows)
        if stage == 0:
            for copy in z_copies[q]:
                copy.wait_recv()
            part = out_ref.at[:, x, core, y, piece]
            peer = x_peer if q % 2 == 0 else y_peer
        else:
            waiting[q].wait_recv()
            started.append(waiting[q])
            if stage == 1 and q % 2 == 0:
                part, peer = out_ref.at[:, :, core, y, piece], y_peer
            elif stage == 1:
                part, peer = out_ref.at[:, x, core, :, piece], x_peer
            else:
                part, peer = out_ref.at[:, :, core, :, piece], core_peer
        if stage < 3:
            waiting[q] = remote(part, part, send.at[q, stage], recv.at[q, stage], peer)
    for copy in w_copies:
        copy.wait_recv()
        started.append(copy)
    for copy in started:
        copy.wait_send()


def gather_rows(normed, weights):
    rows, width = normed.shape
    out, gathered = pl.pallas_call(
        gather_kernel,
        out_shape=(
            jax.ShapeDtypeStruct((4, 2, 2, 2, rows, width), normed.dtype),
            jax.ShapeDtypeStruct(weights.shape, weights.dtype),
        ),
        in_specs=[pl.BlockSpec(memory_space=pltpu.VMEM)] * 2,
        out_specs=(
            pl.BlockSpec(memory_space=pl.ANY),
            pl.BlockSpec(memory_space=pltpu.VMEM),
        ),
        scratch_shapes=[
            pltpu.SemaphoreType.DMA,
            pltpu.SemaphoreType.DMA((PIECES, 3)),
            pltpu.SemaphoreType.DMA((PIECES, 3)),
            pltpu.SemaphoreType.DMA((PIECES, 3)),
            pltpu.SemaphoreType.DMA((PIECES, 3)),
            pltpu.SemaphoreType.DMA((15,)),
            pltpu.SemaphoreType.DMA((15,)),
        ],
        compiler_params=pltpu.CompilerParams(collective_id=0, has_side_effects=True),
    )(normed, weights)
    return out.reshape(-1, width), gathered


def scatter_kernel(
    in_ref, out_ref, in0, in1, in2, in3, sum1, sum2, sum3, z_send, z_recv, send, recv
):
    z, x, core, y = place()
    along_z, x_peer, core_peer, y_peer = peers(z, x, core, y)
    rows = in_ref.shape[4] // PIECES
    f32 = jnp.float32
    greet(along_z, x_peer, core_peer, y_peer)
    started = []
    waiting = []
    for q in range(PIECES):
        part = in_ref.at[:, :, 1 - core, :, pl.ds(q * rows, rows)]
        waiting.append(remote(part, in0.at[q], send.at[q, 0], recv.at[q, 0], core_peer))

    def after_core(q):
        piece = pl.ds(q * rows, rows)

        def add_core(i, carry):
            a, b, c = lax.div(i, 4), lax.rem(lax.div(i, 2), 2), lax.rem(i, 2)
            total = in_ref[a, b, core, c, piece].astype(f32) + in0[q, a, b, c].astype(f32)
            sum1[q, a, b, c] = total.astype(sum1.dtype)
            return carry

        lax.fori_loop(0, 16, add_core, 0)
        if q % 2 == 0:
            part, peer = sum1.at[q, :, 1 - x], x_peer
        else:
            part, peer = sum1.at[q, :, :, 1 - y], y_peer
        return remote(part, in1.at[q], send.at[q, 1], recv.at[q, 1], peer)

    def after_first(q):
        def add_first(i, carry):
            a, b = lax.div(i, 2), lax.rem(i, 2)
            mine = sum1[q, a, x, b] if q % 2 == 0 else sum1[q, a, b, y]
            sum2[q, a, b] = (mine.astype(f32) + in1[q, a, b].astype(f32)).astype(sum2.dtype)
            return carry

        lax.fori_loop(0, 8, add_first, 0)
        if q % 2 == 0:
            part, peer = sum2.at[q, :, 1 - y], y_peer
        else:
            part, peer = sum2.at[q, :, 1 - x], x_peer
        return remote(part, in2.at[q], send.at[q, 2], recv.at[q, 2], peer)

    def after_second(q):
        keep = y if q % 2 == 0 else x

        def add_second(a, carry):
            total = sum2[q, a, keep].astype(f32) + in2[q, a].astype(f32)
            sum3[q, a] = total.astype(sum3.dtype)
            return carry

        lax.fori_loop(0, 4, add_second, 0)
        return [
            remote(
                sum3.at[q, lax.rem(z + i + 1, 4)],
                in3.at[q, i],
                z_send.at[q, i],
                z_recv.at[q, i],
                along_z[i],
            )
            for i in range(3)
        ]

    def after_z(q):
        total = sum3[q, z].astype(f32) + in3[q, 0].astype(f32)
        total = total + (in3[q, 1].astype(f32) + in3[q, 2].astype(f32))
        out_ref[pl.ds(q * rows, rows)] = total

    for turn in range(PIECES + 3):
        for stage in range(4):
            q = turn - stage
            if q < 0 or q >= PIECES:
                continue
            if stage < 3:
                waiting[q].wait_recv()
                started.append(waiting[q])
                waiting[q] = (after_core, after_first, after_second)[stage](q)
            else:
                for copy in waiting[q]:
                    copy.wait_recv()
                    started.append(copy)
                after_z(q)
    for copy in started:
        copy.wait_send()


def scatter_sum(partial):
    rows, width = partial.shape[0] // 32, partial.shape[1]
    piece = (rows // PIECES, width)
    kind = partial.dtype
    return pl.pallas_call(
        scatter_kernel,
        out_shape=jax.ShapeDtypeStruct((rows, width), jnp.float32),
        in_specs=[pl.BlockSpec(memory_space=pltpu.VMEM)],
        out_specs=pl.BlockSpec(memory_space=pltpu.VMEM),
        scratch_shapes=[
            pltpu.VMEM((PIECES, 4, 2, 2, *piece), kind),
            pltpu.VMEM((PIECES, 4, 2, *piece), kind),
            pltpu.VMEM((PIECES, 4, *piece), kind),
            pltpu.VMEM((PIECES, 3, *piece), kind),
            pltpu.VMEM((PIECES, 4, 2, 2, *piece), kind),
            pltpu.VMEM((PIECES, 4, 2, *piece), kind),
            pltpu.VMEM((PIECES, 4, *piece), kind),
            pltpu.SemaphoreType.DMA((PIECES, 3)),
            pltpu.SemaphoreType.DMA((PIECES, 3)),
            pltpu.SemaphoreType.DMA((PIECES, 3)),
            pltpu.SemaphoreType.DMA((PIECES, 3)),
        ],
        compiler_params=pltpu.CompilerParams(
            collective_id=1, has_side_effects=True, vmem_limit_bytes=60 * 1024 * 1024
        ),
    )(partial.reshape(4, 2, 2, 2, rows, width))


def tp_sum_scatter(rows):
    count = lax.axis_size("tp")
    if count != 2:
        return lax.psum_scatter(rows, "tp", scatter_dimension=0, tiled=True)
    me = lax.axis_index("tp")
    each = rows.shape[0] // count
    away = lax.dynamic_slice_in_dim(rows, (1 - me) * each, each, 0).astype(jnp.bfloat16)
    arrived = lax.ppermute(away, "tp", [(0, 1), (1, 0)])
    own = lax.dynamic_slice_in_dim(rows, me * each, each, 0)
    return own + arrived.astype(jnp.float32)


def dense_shards(
    attn,
    o_weight,
    residual,
    norm_gain,
    routes,
    route_logits,
    expert_in,
    expert_out,
    shared_in,
    shared_out,
):
    local_experts = expert_in.shape[0]
    ep_count = lax.axis_size("ep")
    experts = local_experts * ep_count
    ep_me = lax.axis_index("ep")
    weights = route_weights(route_logits)
    chosen = routes[:, :, None] == jnp.arange(experts, dtype=jnp.int32)[None, None, :]
    dense_weights = jnp.sum(jnp.where(chosen, weights[:, :, None], 0.0), axis=1)
    out_weights = jnp.broadcast_to(dense_weights.T[:, None, :], (experts, 8, routes.shape[0]))

    attn_out = tp_sum_scatter(jnp.dot(attn, o_weight, preferred_element_type=jnp.float32))
    hidden = residual.astype(jnp.float32) + attn_out
    inv_norm = lax.rsqrt(jnp.mean(hidden * hidden, axis=-1, keepdims=True) + 1e-06)
    normed = (hidden * inv_norm * norm_gain).astype(jnp.bfloat16)
    all_rows, all_weights = gather_rows(normed, out_weights)
    my_weights = all_weights[:, 0, :].reshape(-1, 1)
    group = routes.shape[0]
    group_rows = lax.dynamic_slice_in_dim(all_rows, ep_me * group, group, 0)
    shared = shared_part(group_rows, shared_in, shared_out)
    partial = None
    for item in range(local_experts):
        gate_val = jnp.dot(all_rows, expert_in[item, 0], preferred_element_type=jnp.float32)
        up_val = jnp.dot(all_rows, expert_in[item, 1], preferred_element_type=jnp.float32)
        active = (jax.nn.silu(gate_val) * up_val).astype(jnp.bfloat16)
        value = jnp.einsum("tf,df->td", active, expert_out[item], preferred_element_type=jnp.float32)
        value = value * my_weights[:, item : item + 1]
        partial = value if partial is None else partial + value
    partial = partial.astype(jnp.bfloat16)
    own = lax.dynamic_slice_in_dim(partial, ep_me * group, group, 0).astype(jnp.float32) + shared
    partial = lax.dynamic_update_slice_in_dim(
        partial, own.astype(jnp.bfloat16), ep_me * group, 0
    )
    return (hidden + scatter_sum(partial)).astype(jnp.bfloat16)


def shards(*args):
    routes, expert_in = args[4], args[6]
    experts = expert_in.shape[0] * lax.axis_size("ep")
    spans = lax.axis_size("ep") == 16 and lax.axis_size("tp") == 2
    if spans and experts <= 4 * routes.shape[1]:
        return dense_shards(*args)
    return slotted_shards(*args)


def solution(mesh):
    in_specs = (
        P("ep", "tp"),
        P("tp", None),
        P(("ep", "tp"), None),
        P(),
        P("ep", None),
        P("ep", None),
        P("ep", None, None, "tp"),
        P("ep", None, "tp"),
        P(None, None, "tp"),
        P(None, "tp"),
    )
    out_specs = P(("ep", "tp"), None)
    return jax.shard_map(shards, mesh=mesh, in_specs=in_specs, out_specs=out_specs, check_vma=False)
```

profile of v0, /device:TPU:0, one launch (start us, length us, event | category | flops | bytes accessed | tf_op | source)
XLA Modules:
  0.0 184.9 jit_solution(4458575927542361870)
XLA Ops:
  0.0 0.0 copy-start
  0.0 0.0 copy-start.2
  0.0 0.0 copy-start.4
  0.0 0.0 copy-start.3
  0.0 3.1 %fusion.40 = f32[128,2048]{1,0:T(8,128)S(1)} fusion(bf16[128,1024]{1,0:T(8,128)(2,1)} %param.10, bf16[1024,2048]{1,0:T(8,128)(2,1)} %param.11), kind=kOutput, calls=%fused_computation.43 | convolution fusion | flops 536870912 | bytes 5505024 | tf_op jit(solution)/shard_map/dot_general | solution.py:383
  3.2 0.0 copy-start.1
  3.2 1.0 copy-done.1
  4.2 3.1 %collective-permute-start = (bf16[64,2048]{1,0:T(8,128)(2,1)S(1)}, bf16[64,2048]{1,0:T(8,128)(2,1)}, u32[]{:S(2)}, u32[]{:S(2)}) collective-permute-start(bf16[64,2048]{1,0:T(8,128)(2,1)S(1)} %dynamic-slice_convert_fusion), channel_id=1, source_target_pairs={{0,1},{1,0},{2,3},{3,2},{4,5},{5,4},{6,7},{7,6},{8,9},{9,8},{10,11... | collective-permute-start | bytes 786440 | tf_op jit(solution)/shard_map/ppermute | solution.py:357
  7.2 0.0 copy-done.2
  7.3 0.0 copy-done.4
  7.3 6.3 %collective-permute-done = bf16[64,2048]{1,0:T(8,128)(2,1)} collective-permute-done((bf16[64,2048]{1,0:T(8,128)(2,1)S(1)}, bf16[64,2048]{1,0:T(8,128)(2,1)}, u32[]{:S(2)}, u32[]{:S(2)}) %collective-permute-start) | collective-permute-done | bytes 262176 | tf_op jit(solution)/shard_map/ppermute | solution.py:357
  13.7 1.4 multiply_reduce_fusion
  15.1 0.0 copy-done.3
  15.1 0.8 multiply_convert_fusion.2.in_ref
  15.9 0.6 broadcast_in_dim.16.w_ref
  16.5 62.6 %shard_map.100 = (bf16[4,2,2,2,64,2048]{5,4,3,2,1,0:T(8,128)(2,1)}, f32[16,8,128]{2,1,0:T(8,128)}) custom-call(bf16[64,2048]{1,0:T(8,128)(2,1)} %multiply_convert_fusion.2.in_ref, f32[16,8,128]{2,1,0:T(8,128)} %broadcast_in_dim.16.w_ref), custom_call_target="tpu_custom_call" | custom-call | tf_op jit(solution)/shard_map/pallas_call | solution.py:210
  79.1 0.8 slice.17
  80.0 11.8 %fusion.7 = f32[2048,704]{0,1:T(8,128)} fusion(bf16[2048,2048]{1,0:T(8,128)(2,1)} %bitcast.34, bf16[1,2,2048,704]{2,3,1,0:T(8,128)(2,1)} %param.16), kind=kOutput, calls=%fused_computation.8 | convolution fusion | flops 5905580032 | bytes 17039360 | tf_op jit(solution)/shard_map/dot_general | solution.py:394
  91.8 3.6 %fusion.2 = f32[128,704]{0,1:T(8,128)} fusion(bf16[2,2048,704]{1,2,0:T(8,128)(2,1)} %param.18, bf16[2048,2048]{1,0:T(8,128)(2,1)} %bitcast.35, s32[]{:T(128)S(6)} %select_n.18), kind=kOutput, calls=%fused_computation.4 | convolution fusion | flops 369098752 | bytes 3768324 | tf_op jit(solution)/shard_map/dot_general | solution.py:41
  95.4 0.0 copy-done
  95.4 19.1 %multiply_convert_fusion = bf16[2048,2048]{1,0:T(8,128)(2,1)} fusion(f32[2048]{0:T(1024)S(1)} %bitcast.33, f32[2048,704]{0,1:T(8,128)} %fusion.7, bf16[2048,2048]{1,0:T(8,128)(2,1)} %bitcast.36, bf16[1,2048,704]{1,2,0:T(8,128)(2,1)S(1)} %copy-done, bf16[1,2,2048,704]{2,3,1,0:T(8,128)(2,1)} %param.16), kind=kOutput, calls=%fused_computation | convolution fusion | flops 11828199424 | bytes 28319744 | tf_op jit(solution)/shard_map/tf,df->td/dot_general | solution.py:397
  114.5 6.0 %fusion.16 = bf16[2048,2048]{1,0:T(8,128)(2,1)} fusion(bf16[2048,2048]{1,0:T(8,128)(2,1)} %multiply_convert_fusion, s32[]{:T(128)S(6)} %select_n.18, bf16[2048,704]{0,1:T(8,128)(2,1)} %param.19, bf16[2,2048,704]{1,2,0:T(8,128)(2,1)} %param.18, bf16[2048,2048]{1,0:T(8,128)(2,1)} %bitcast.37, f32[128,704]{0,1:T(8,128)} %fusion.2), kind=kOutput, calls=%fused_computation.17 | convolution fusion | flops 739524608 | bytes 7701504 | tf_op jit(solution)/shard_map/tf,df->td/dot_general | solution.py:44
  120.5 62.6 %shard_map.101 = f32[64,2048]{1,0:T(8,128)} custom-call(bf16[4,2,2,2,64,2048]{5,4,3,2,1,0:T(8,128)(2,1)} %bitcast.31), custom_call_target="tpu_custom_call" | custom-call | tf_op jit(solution)/shard_map/pallas_call | solution.py:326
  183.1 1.8 add_convert_fusion
  (5 shorter events, 0.1 us)
Async XLA Ops:
  0.0 95.4 %copy-start = (bf16[1,2048,704]{1,2,0:T(8,128)(2,1)S(1)}, bf16[1,2048,704]{1,2,0:T(8,128)(2,1)}, u32[]{:S(2)}) copy-start(bf16[1,2048,704]{1,2,0:T(8,128)(2,1)} %param.17) | copy-start | bytes 8650756
  0.0 7.2 %copy-start.2 = (f32[128,6]{0,1:T(8,128)S(1)}, f32[128,6]{0,1:T(8,128)}, u32[]{:S(2)}) copy-start(f32[128,6]{0,1:T(8,128)} %param.15) | copy-start | bytes 9220
  0.0 7.3 %copy-start.4 = (s32[128,6]{0,1:T(8,128)S(1)}, s32[128,6]{0,1:T(8,128)}, u32[]{:S(2)}) copy-start(s32[128,6]{0,1:T(8,128)} %param.14) | copy-start | bytes 9220
  0.0 15.1 %copy-start.3 = (f32[2048]{0:T(1024)S(1)}, f32[2048]{0:T(1024)}, u32[]{:S(2)}) copy-start(f32[2048]{0:T(1024)} %param.13) | copy-start | bytes 24580
  3.2 1.0 copy-start.1
  4.2 9.5 %collective-permute-start = (bf16[64,2048]{1,0:T(8,128)(2,1)S(1)}, bf16[64,2048]{1,0:T(8,128)(2,1)}, u32[]{:S(2)}, u32[]{:S(2)}) collective-permute-start(bf16[64,2048]{1,0:T(8,128)(2,1)S(1)} %dynamic-slice_convert_fusion), channel_id=1, source_target_pairs={{0,1},{1,0},{2,3},{3,2},{4,5},{5,4},{6,7},{7,6},{8,9},{9,8},{10,11... | collective-permute-start | bytes 786440 | tf_op jit(solution)/shard_map/ppermute | solution.py:357
where the time goes:
time: 185 us
  Pallas kernels  125 us (68%)
  matrix products  43.6 us (24%)
  waiting for transfers between devices  6.34 us (3%)
  other arithmetic  4.07 us (2%)
  starting transfers between devices  3.07 us (2%)
  local copies, waits for them, and re-layouts  2.51 us (1%)
    pallas_call x1, Pallas kernels, scatter_sum(): pl.pallas_call(scatter_kernel, out_shape=jax.ShapeDtypeStruct((rows, widt...  62.6 us
    pallas_call x1, Pallas kernels, gather_rows(): pl.pallas_call(gather_kernel, out_shape=(jax.ShapeDtypeStruct((4, 2, 2, 2...  62.6 us
    dot_general x1, matrix products, dense_shards(): jnp.einsum('tf,df->td', active, expert_out[item], preferred_element_type=...  19.1 us
    dot_general x1, matrix products, dense_shards(): jnp.dot(all_rows, expert_in[item, 0], preferred_element_type=jnp.float32)  11.8 us
    ppermute x1, waiting for transfers between devices, tp_sum_scatter(): arrived = lax.ppermute(away, 'tp', [(0, 1), (1, 0)])  6.34 us
    dot_general x1, matrix products, shared_part(): jnp.einsum('tf,df->td', active, s_out, preferred_element_type=jnp.float32)  6 us
  transfers between devices with their start and end apart: 1, of which 1 were waited for; matrix products, arithmetic and copies ran while one was open for 0% of the time, Pallas kernels for 0%

commit v1 on v0

v1 whole, which is shorter than its diff:
```python
import jax
import jax.numpy as jnp
from jax import lax
from jax.experimental import pallas as pl
from jax.experimental.pallas import tpu as pltpu
from jax.sharding import PartitionSpec as P

PIECES = 4
PIECE_ROWS = 16
TRACKS = (
    (0, 640, "zxy"),
    (640, 640, "zyx"),
    (1280, 384, "xzy"),
    (1664, 384, "yzx"),
)
HIDDEN_TILES = 256
OUT_TILES = 256


def slot_places(route_rows, capacity, experts):
    flat_routes = route_rows.reshape(-1)
    onehot = (flat_routes[:, None] == jnp.arange(experts, dtype=jnp.int32)[None, :]).astype(
        jnp.int32
    )
    before = jnp.cumsum(onehot, axis=0) - onehot
    ranks = jnp.sum(before * onehot, axis=1)
    return flat_routes * capacity + ranks


def fill_slots(source_rows, places, capacity, experts, topk):
    copies = jnp.repeat(source_rows, topk, axis=0)
    empty_slots = jnp.zeros((experts * capacity, source_rows.shape[1]), source_rows.dtype)
    return empty_slots.at[places].set(copies)


def route_weights(logits):
    sigmoids = jax.nn.sigmoid(logits)
    return 2.446 * sigmoids / jnp.sum(sigmoids, axis=-1, keepdims=True)


def expert_part(slots, w_in, w_out):
    gate_val = jnp.einsum("slcd,ldf->slcf", slots, w_in[:, 0], preferred_element_type=jnp.float32)
    up_val = jnp.einsum("slcd,ldf->slcf", slots, w_in[:, 1], preferred_element_type=jnp.float32)
    active = (jax.nn.silu(gate_val) * up_val).astype(jnp.bfloat16)
    return jnp.einsum("slcf,ldf->slcd", active, w_out, preferred_element_type=jnp.float32)


def shared_part(source_rows, s_in, s_out):
    gate_val = jnp.dot(source_rows, s_in[0], preferred_element_type=jnp.float32)
    up_val = jnp.dot(source_rows, s_in[1], preferred_element_type=jnp.float32)
    active = (jax.nn.silu(gate_val) * up_val).astype(jnp.bfloat16)
    return jnp.einsum("tf,df->td", active, s_out, preferred_element_type=jnp.float32)


def combine_slots(values, places, weights, topk):
    picked = values[places].reshape(-1, topk, values.shape[1])
    return jnp.sum(picked * weights[:, :, None], axis=1)


def slotted_shards(
    attn,
    o_weight,
    residual,
    norm_gain,
    routes,
    route_logits,
    expert_in,
    expert_out,
    shared_in,
    shared_out,
):
    tok_rows = residual.shape[0]
    width = residual.shape[1]
    topk = routes.shape[1]
    tp_count = lax.axis_size("tp")
    ep_count = lax.axis_size("ep")
    local_experts = expert_in.shape[0]
    experts = local_experts * ep_count
    capacity = max(2, (4 * tok_rows * topk + 3 * experts - 1) // (3 * experts))
    attn_out = lax.psum_scatter(
        jnp.dot(attn, o_weight, preferred_element_type=jnp.float32),
        "tp",
        scatter_dimension=0,
        tiled=True,
    )
    hidden = residual.astype(jnp.float32) + attn_out
    inv_norm = lax.rsqrt(jnp.mean(hidden * hidden, axis=-1, keepdims=True) + 1e-06)
    normed = (hidden * inv_norm * norm_gain).astype(jnp.bfloat16)
    group_rows = lax.all_gather(normed, "tp", axis=0, tiled=True)
    group_cap = tp_count * capacity
    places = slot_places(routes, group_cap, experts)
    outgoing = fill_slots(group_rows, places, group_cap, experts, topk)
    incoming = lax.all_to_all(outgoing, "ep", split_axis=0, concat_axis=0, tiled=True)
    partial_value = expert_part(
        incoming.reshape(ep_count, local_experts, group_cap, width), expert_in, expert_out
    )
    returned = lax.all_to_all(
        partial_value.reshape(-1, width), "ep", split_axis=0, concat_axis=0, tiled=True
    )
    mixture = combine_slots(returned, places, route_weights(route_logits), topk)
    mixture = mixture + shared_part(group_rows, shared_in, shared_out)
    moe_sum = lax.psum_scatter(mixture, "tp", scatter_dimension=0, tiled=True)
    return (hidden + moe_sum).astype(jnp.bfloat16)


def place():
    ep = lax.axis_index("ep")
    return lax.div(ep, 4), lax.rem(lax.div(ep, 2), 2), lax.rem(ep, 2), lax.axis_index("tp")


def device_at(z, x, core, y):
    return (z * 4 + x * 2 + core, y)


def peers(z, x, core, y):
    along_z = [device_at(lax.rem(z + step, 4), x, core, y) for step in (1, 2, 3)]
    return (
        along_z,
        device_at(z, 1 - x, core, y),
        device_at(z, x, 1 - core, y),
        device_at(z, x, core, 1 - y),
    )


def remote(src, dst, send_sem, recv_sem, peer):
    return pltpu.make_async_remote_copy(
        src_ref=src,
        dst_ref=dst,
        send_sem=send_sem,
        recv_sem=recv_sem,
        device_id=peer,
        device_id_type=pl.DeviceIdType.MESH,
    )


def tiles(total, step):
    return [(start, min(step, total - start)) for start in range(0, total, step)]


def fused_kernel(
    attn_ref,
    gain_ref,
    residual_ref,
    w_ref,
    o_hbm,
    ein_hbm,
    eout_hbm,
    sin_hbm,
    sout_hbm,
    out_ref,
    o_vmem,
    ein,
    eout,
    s_in,
    s_out,
    products,
    hidden,
    away,
    arrived,
    rows_all,
    partial,
    core_in,
    w_all,
    w_cols,
    active,
    shared_active,
    shared_sum,
    *rest,
):
    boxes = rest[: 3 * len(TRACKS)]
    (
        load_sem,
        w_send,
        w_recv,
        y_send,
        y_recv,
        g_send,
        g_recv,
        gc_send,
        gc_recv,
        s_send,
        s_recv,
        sc_send,
        sc_recv,
    ) = rest[3 * len(TRACKS) :]
    f32, bf16 = jnp.float32, jnp.bfloat16
    z, x, core, y = place()
    along_z, x_peer, core_peer, y_peer = peers(z, x, core, y)
    ep = lax.axis_index("ep")
    mine = {"z": z, "x": x, "y": y}
    width = out_ref.shape[1]
    half = out_ref.shape[0]
    piece_total = 32 * PIECE_ROWS

    o_tiles = tiles(width, 512)
    o_loads = [
        pltpu.make_async_copy(
            o_hbm.at[:, pl.ds(start, size)], o_vmem.at[:, pl.ds(start, size)], load_sem.at[i]
        )
        for i, (start, size) in enumerate(o_tiles)
    ]
    weight_loads = [
        pltpu.make_async_copy(src, dst, load_sem.at[len(o_tiles) + i])
        for i, (src, dst) in enumerate(
            ((sin_hbm, s_in), (sout_hbm, s_out), (ein_hbm.at[0], ein), (eout_hbm.at[0], eout))
        )
    ]
    for copy in o_loads:
        copy.start()

    others = [lax.rem(ep + step, 16) for step in range(1, 16)]
    barrier = pltpu.get_barrier_semaphore()
    for peer in [(other, y) for other in others] + [y_peer]:
        pl.semaphore_signal(barrier, inc=1, device_id=peer, device_id_type=pl.DeviceIdType.MESH)

    for i, (start, size) in enumerate(o_tiles):
        o_loads[i].wait()
        products[:, start : start + size] = jnp.dot(
            attn_ref[...], o_vmem[:, start : start + size], preferred_element_type=f32
        )
    for copy in weight_loads:
        copy.start()
    for q in range(PIECES):
        away[q] = products[pl.ds((1 - y) * half + q * PIECE_ROWS, PIECE_ROWS), :].astype(bf16)

    pl.semaphore_wait(barrier, 16)

    def y_copy(q):
        return remote(away.at[q], arrived.at[q], y_send.at[q], y_recv.at[q], y_peer)

    for q in range(PIECES):
        y_copy(q).start()
    w_copies = [
        remote(w_ref.at[other], w_all.at[ep], w_send.at[i], w_recv.at[i], (other, y))
        for i, other in enumerate(others)
    ]
    for copy in w_copies:
        copy.start()
    w_all[ep] = w_ref[ep]

    def block(ref, q, index, cols):
        return ref.at[q, index["z"], index["x"], core, index["y"], :, cols]

    every = {"z": pl.ds(0, 4), "x": pl.ds(0, 2), "y": pl.ds(0, 2)}

    def gather_copies(q, track, stage):
        start, size, order = TRACKS[track]
        done, axis = order[:stage], order[stage]
        index = {a: every[a] if a in done else mine[a] for a in "zxy"}
        part = block(rows_all, q, index, pl.ds(start, size))
        slot = track * 5 + stage + (2 if "z" in done else 0)
        targets = along_z if axis == "z" else [x_peer if axis == "x" else y_peer]
        return [
            remote(part, part, g_send.at[q, slot + i], g_recv.at[q, slot + i], target)
            for i, target in enumerate(targets)
        ]

    def gather_core(q):
        part = rows_all.at[q, :, :, core]
        return remote(part, part, gc_send.at[q], gc_recv.at[q], core_peer)

    def scatter_core(q):
        return remote(
            partial.at[q, :, :, 1 - core], core_in.at[q], sc_send.at[q], sc_recv.at[q], core_peer
        )

    def scatter_index(track, stage, value):
        order = TRACKS[track][2][::-1]
        index = {a: every[a] for a in order[stage + 1 :]}
        index.update({a: mine[a] for a in order[:stage]})
        index[order[stage]] = value
        return index

    def scatter_copies(q, track, stage):
        start, size, order = TRACKS[track]
        axis = order[2 - stage]
        box = boxes[3 * track + stage]
        slot = track * 5 + stage + (2 if "z" in order[3 - stage :] else 0)
        if axis == "z":
            targets = [(along_z[i], lax.rem(z + i + 1, 4), box.at[q, i]) for i in range(3)]
        else:
            targets = [(x_peer if axis == "x" else y_peer, 1 - mine[axis], box.at[q, 0])]
        return [
            remote(
                block(partial, q, scatter_index(track, stage, value), pl.ds(start, size)),
                dst,
                s_send.at[q, slot + i],
                s_recv.at[q, slot + i],
                target,
            )
            for i, (target, value, dst) in enumerate(targets)
        ]

    def start_gather(q):
        y_copy(q).wait_recv()
        at = pl.multiple_of(q * PIECE_ROWS, PIECE_ROWS)
        own = pl.multiple_of(y * half + q * PIECE_ROWS, PIECE_ROWS)
        total = residual_ref[pl.ds(at, PIECE_ROWS), :].astype(f32)
        total = total + (products[pl.ds(own, PIECE_ROWS), :] + arrived[q].astype(f32))
        hidden[pl.ds(at, PIECE_ROWS), :] = total
        inv_norm = lax.rsqrt(jnp.mean(total * total, axis=-1, keepdims=True) + 1e-06)
        rows_all[q, z, x, core, y] = (total * inv_norm * gain_ref[...]).astype(bf16)
        for track in range(len(TRACKS)):
            for copy in gather_copies(q, track, 0):
                copy.start()

    def step_gather(stage):
        def step(q):
            for track in range(len(TRACKS)):
                for copy in gather_copies(q, track, stage - 1):
                    copy.wait_recv()
                if stage < 3:
                    for copy in gather_copies(q, track, stage):
                        copy.start()
            if stage == 3:
                gather_core(q).start()

        return step

    def end_gather(q):
        gather_core(q).wait_recv()

    def gate_up(rows, w_in, start, size):
        gate = jnp.dot(rows, w_in[0, :, start : start + size], preferred_element_type=f32)
        up = jnp.dot(rows, w_in[1, :, start : start + size], preferred_element_type=f32)
        return jax.nn.silu(gate) * up

    def down(act, w_out, start, size):
        return lax.dot_general(
            act, w_out[start : start + size, :], (((1,), (1,)), ((), ())),
            preferred_element_type=f32,
        )

    hidden_tiles = tiles(ein.shape[2], HIDDEN_TILES)
    out_tiles = tiles(width, OUT_TILES)

    def expert_in_tile(i):
        def step(q):
            start, size = hidden_tiles[i]
            rows = rows_all[q].reshape(piece_total, width)
            value = gate_up(rows, ein, start, size) * w_cols[q][:, 0:1]
            active[:, start : start + size] = value.astype(bf16)

        return step

    def expert_out_tiles(chosen):
        def step(q):
            for start, size in chosen:
                value = down(active[...], eout, start, size).astype(bf16)
                partial[q, :, :, :, :, :, start : start + size] = value.reshape(
                    4, 2, 2, 2, PIECE_ROWS, size
                )

        return step

    def shared_rows(q):
        rows = rows_all[q, z, x, core].reshape(2 * PIECE_ROWS, width)
        for start, size in hidden_tiles:
            shared_active[:, start : start + size] = gate_up(rows, s_in, start, size).astype(bf16)
        for start, size in out_tiles:
            shared_sum[:, start : start + size] = down(shared_active[...], s_out, start, size)

    def start_scatter(q):
        own = partial[q, z, x, core].reshape(2 * PIECE_ROWS, width).astype(f32) + shared_sum[...]
        partial[q, z, x, core] = own.astype(bf16).reshape(2, PIECE_ROWS, width)
        scatter_core(q).start()

    def after_core(q):
        scatter_core(q).wait_recv()

        def add(i, carry):
            a, b, c = lax.div(i, 4), lax.rem(lax.div(i, 2), 2), lax.rem(i, 2)
            total = partial[q, a, b, core, c].astype(f32) + core_in[q, a, b, c].astype(f32)
            partial[q, a, b, core, c] = total.astype(bf16)
            return carry

        lax.fori_loop(0, 16, add, 0)
        for track in range(len(TRACKS)):
            for copy in scatter_copies(q, track, 0):
                copy.start()

    def after_stage(stage):
        def step(q):
            for track in range(len(TRACKS)):
                start, size, order = TRACKS[track]
                cols = pl.ds(start, size)
                axis = order[2 - stage]
                left = [a for a in "zxy" if a in order[: 2 - stage]]
                box = boxes[3 * track + stage]
                for copy in scatter_copies(q, track, stage):
                    copy.wait_recv()
                counts = [4 if a == "z" else 2 for a in left]
                number = 1
                for count in counts:
                    number = number * count

                def add(i, carry):
                    index = dict(mine)
                    inner = []
                    rest_of = i
                    for a, count in reversed(list(zip(left, counts))):
                        index[a] = lax.rem(rest_of, count)
                        rest_of = lax.div(rest_of, count)
                        inner.insert(0, index[a])
                    at = (q, index["z"], index["x"], core, index["y"], slice(None), cols)
                    total = partial[at].astype(f32)
                    for j in range(3 if axis == "z" else 1):
                        total = total + box[(q, j, *inner)].astype(f32)
                    if stage == 2:
                        rows = pl.ds(pl.multiple_of(q * PIECE_ROWS, PIECE_ROWS), PIECE_ROWS)
                        out_ref[rows, cols] = (hidden[rows, cols] + total).astype(bf16)
                    else:
                        partial[at] = total.astype(bf16)
                    return carry

                if number == 1:
                    add(0, 0)
                else:
                    lax.fori_loop(0, number, add, 0)
                if stage < 2:
                    for copy in scatter_copies(q, track, stage + 1):
                        copy.start()

        return step

    start_gather(0)
    start_gather(1)

    for copy in w_copies:
        copy.wait_recv()
    turned = jnp.transpose(w_all[...].reshape(128, 128))
    for q in range(PIECES):
        for e in range(16):
            for b in range(2):
                at = e * 2 * PIECE_ROWS + b * PIECE_ROWS
                source = b * half + q * PIECE_ROWS
                w_cols[q, at : at + PIECE_ROWS, :] = jnp.broadcast_to(
                    turned[source : source + PIECE_ROWS, e * 8 : e * 8 + 1], (PIECE_ROWS, 128)
                )
    for copy in weight_loads:
        copy.wait()

    middle = len(out_tiles) // 2
    plan = [
        (-3, end_gather),
        (-3, expert_in_tile(0)),
        (-4, after_core),
        (-3, expert_in_tile(1)),
        (0, step_gather(1)),
        (2, start_gather),
        (-3, expert_in_tile(2)),
        (-1, step_gather(2)),
        (-3, expert_out_tiles(out_tiles[:middle])),
        (-5, after_stage(0)),
        (-2, step_gather(3)),
        (-3, expert_out_tiles(out_tiles[middle:])),
        (-3, start_scatter),
        (-6, after_stage(1)),
        (-7, after_stage(2)),
        (-2, shared_rows),
    ]
    turns = PIECES - min(shift for shift, _ in plan)

    def turn(u, carry):
        for shift, step in plan:
            q = u + shift

            @pl.when(jnp.logical_and(q >= 0, q < PIECES))
            def run(step=step, q=q):
                step(q)

        return carry

    lax.fori_loop(0, turns, turn, 0)

    def finish(q, carry):
        y_copy(q).wait_send()
        gather_core(q).wait_send()
        scatter_core(q).wait_send()
        for track in range(len(TRACKS)):
            for stage in range(3):
                for copy in gather_copies(q, track, stage) + scatter_copies(q, track, stage):
                    copy.wait_send()
        return carry

    lax.fori_loop(0, PIECES, finish, 0)
    for copy in w_copies:
        copy.wait_send()


def fused(attn, gain, residual, weights, o_weight, expert_in, expert_out, shared_in, shared_out):
    rows, width = residual.shape
    hidden_units = expert_in.shape[3]
    bf16, f32 = jnp.bfloat16, jnp.float32
    boxes = []
    for _, size, order in TRACKS:
        for stage in range(3):
            left = [4 if a == "z" else 2 for a in "zxy" if a in order[: 2 - stage]]
            boxes.append(
                pltpu.VMEM(
                    (PIECES, 3 if order[2 - stage] == "z" else 1, *left, PIECE_ROWS, size), bf16
                )
            )
    dma = pltpu.SemaphoreType.DMA
    slots = 5 * len(TRACKS)
    vmem = pl.BlockSpec(memory_space=pltpu.VMEM)
    hbm = pl.BlockSpec(memory_space=pl.ANY)
    return pl.pallas_call(
        fused_kernel,
        out_shape=jax.ShapeDtypeStruct((rows, width), bf16),
        in_specs=[vmem] * 4 + [hbm] * 5,
        out_specs=vmem,
        scratch_shapes=[
            pltpu.VMEM(o_weight.shape, bf16),
            pltpu.VMEM(expert_in.shape[1:], bf16),
            pltpu.VMEM(expert_out.shape[1:], bf16),
            pltpu.VMEM(shared_in.shape, bf16),
            pltpu.VMEM(shared_out.shape, bf16),
            pltpu.VMEM((2 * rows, width), f32),
            pltpu.VMEM((rows, width), f32),
            pltpu.VMEM((PIECES, PIECE_ROWS, width), bf16),
            pltpu.VMEM((PIECES, PIECE_ROWS, width), bf16),
            pltpu.VMEM((PIECES, 4, 2, 2, 2, PIECE_ROWS, width), bf16),
            pltpu.VMEM((PIECES, 4, 2, 2, 2, PIECE_ROWS, width), bf16),
            pltpu.VMEM((PIECES, 4, 2, 2, PIECE_ROWS, width), bf16),
            pltpu.VMEM((16, 8, 128), f32),
            pltpu.VMEM((PIECES, 32 * PIECE_ROWS, 128), f32),
            pltpu.VMEM((32 * PIECE_ROWS, hidden_units), bf16),
            pltpu.VMEM((2 * PIECE_ROWS, hidden_units), bf16),
            pltpu.VMEM((2 * PIECE_ROWS, width), f32),
            *boxes,
            dma((8,)),
            dma((15,)),
            dma((15,)),
            dma((PIECES,)),
            dma((PIECES,)),
            dma((PIECES, slots)),
            dma((PIECES, slots)),
            dma((PIECES,)),
            dma((PIECES,)),
            dma((PIECES, slots)),
            dma((PIECES, slots)),
            dma((PIECES,)),
            dma((PIECES,)),
        ],
        compiler_params=pltpu.CompilerParams(
            collective_id=0, has_side_effects=True, vmem_limit_bytes=60 * 1024 * 1024
        ),
    )(attn, gain, residual, weights, o_weight, expert_in, expert_out, shared_in, shared_out)


def fused_shards(
    attn,
    o_weight,
    residual,
    norm_gain,
    routes,
    route_logits,
    expert_in,
    expert_out,
    shared_in,
    shared_out,
):
    experts = expert_in.shape[0] * lax.axis_size("ep")
    weights = route_weights(route_logits)
    chosen = routes[:, :, None] == jnp.arange(experts, dtype=jnp.int32)[None, None, :]
    dense_weights = jnp.sum(jnp.where(chosen, weights[:, :, None], 0.0), axis=1)
    out_weights = jnp.broadcast_to(dense_weights.T[:, None, :], (experts, 8, routes.shape[0]))
    return fused(
        attn,
        norm_gain[None, :],
        residual,
        out_weights,
        o_weight,
        expert_in,
        expert_out,
        shared_in,
        shared_out,
    )


def shards(*args):
    routes, expert_in = args[4], args[6]
    experts = expert_in.shape[0] * lax.axis_size("ep")
    spans = lax.axis_size("ep") == 16 and lax.axis_size("tp") == 2
    fits = args[2].shape[0] == PIECES * PIECE_ROWS and expert_in.shape[0] == 1
    if spans and fits and experts <= 4 * routes.shape[1]:
        return fused_shards(*args)
    return slotted_shards(*args)


def solution(mesh):
    in_specs = (
        P("ep", "tp"),
        P("tp", None),
        P(("ep", "tp"), None),
        P(),
        P("ep", None),
        P("ep", None),
        P("ep", None, None, "tp"),
        P("ep", None, "tp"),
        P(None, None, "tp"),
        P(None, "tp"),
    )
    out_specs = P(("ep", "tp"), None)
    return jax.shard_map(shards, mesh=mesh, in_specs=in_specs, out_specs=out_specs, check_vma=False)
```

time: 185 us -> 132 us (0.71)
  matrix products: 43.6 us -> 0 us
  local copies, waits for them, and re-layouts: 2.51 us -> 26.8 us
  Pallas kernels: 125 us -> 102 us
  waiting for transfers between devices: 6.34 us -> 0 us
  starting transfers between devices: 3.07 us -> 0 us
    dot_general x5 -> x0, matrix products: 43.6 us -> none  [the longest x1 19.1 us: dense_shards(): jnp.einsum('tf,df->td', active, expert_out[item], preferred_element_type=...]
    unnamed x10 -> x7, local copies, waits for them, and re-layouts: 1 us -> 26.2 us
    pallas_call x2 -> x1, Pallas kernels: 125 us -> 102 us  [fused(): pl.pallas_call(fused_kernel, out_shape=jax.ShapeDtypeStruct((rows, width)...]
    ppermute x1 -> x0, waiting for transfers between devices: 6.34 us -> none  [tp_sum_scatter(): arrived = lax.ppermute(away, 'tp', [(0, 1), (1, 0)])]
    ppermute x1 -> x0, starting transfers between devices: 3.07 us -> none  [tp_sum_scatter(): arrived = lax.ppermute(away, 'tp', [(0, 1), (1, 0)])]
    convert_element_type x2 -> x0, other arithmetic: 2.62 us -> none  [the longest x1 1.8 us: dense_shards(): return (hidden + scatter_sum(partial)).astype(jnp.bfloat16)]
  transfers between devices with their start and end apart: 1 -> 0, of which waited for: 1 -> 0; matrix products, arithmetic and copies ran while one was open for 0% -> 0% of each run, Pallas kernels for 0% -> 0%
where the time goes in v1:
time: 132 us; the launch traced here: 131 us
  Pallas kernels  102 us (77%)
  local copies, waits for them, and re-layouts  26.8 us (20%)
  other arithmetic  2.28 us (2%)
    pallas_call x1, Pallas kernels, fused(): pl.pallas_call(fused_kernel, out_shape=jax.ShapeDtypeStruct((rows, width)...  102 us
    unnamed x7, local copies, waits for them, and re-layouts  26.2 us

profile of v1, /device:TPU:0, one launch (start us, length us, event | category | flops | bytes accessed | tf_op | source)
XLA Modules:
  0.0 131.5 jit_solution(12260066203239002268)
XLA Ops:
  0.0 0.0 copy-start
  0.0 0.9 fusion
  0.9 0.7 multiply_divide_fusion
  1.6 0.7 select_reduce_fusion
  2.3 0.6 broadcast_in_dim.28.w_ref
  2.9 4.6 %copy.18.eout_hbm = bf16[1,2048,704]{2,1,0:T(8,128)(2,1)} copy(bf16[1,2048,704]{1,2,0:T(8,128)(2,1)} %param.17) | data formatting | bytes 5767168 | tf_op args[7]
  7.6 0.0 copy-done
  7.6 2.9 %copy.20.sout_hbm = bf16[2048,704]{1,0:T(8,128)(2,1)} copy(bf16[2048,704]{0,1:T(8,128)(2,1)S(1)} %copy-done) | data formatting | bytes 5767168 | tf_op args[9]
  10.4 8.5 %copy.17.ein_hbm = bf16[1,2,2048,704]{3,2,1,0:T(8,128)(2,1)} copy(bf16[1,2,2048,704]{2,3,1,0:T(8,128)(2,1)} %param.16) | data formatting | bytes 11534336 | tf_op args[6]
  19.0 8.5 %copy.19.sin_hbm = bf16[2,2048,704]{2,1,0:T(8,128)(2,1)} copy(bf16[2,2048,704]{1,2,0:T(8,128)(2,1)} %param.18) | data formatting | bytes 11534336 | tf_op args[8]
  27.4 102.4 %shard_map.100 = bf16[64,2048]{1,0:T(8,128)(2,1)} custom-call(bf16[128,1024]{1,0:T(8,128)(2,1)} %attn_ref.1, f32[1,2048]{1,0:T(1,128)} %bitcast.3, bf16[64,2048]{1,0:T(8,128)(2,1)} %residual_ref.1, f32[16,8,128]{2,1,0:T(8,128)} %broadcast_in_dim.28.w_ref, bf16[1024,2048]{1,0:T(8,128)(2,1)} %o_hbm.1, bf16[1,2,2048,704]{3,2,1,0:T(8,128)(2,1)} %copy.17.ein_hbm, ...), custom_call_target="tpu_custom_call" | custom-call | tf_op jit(solution)/shard_map/pallas_call | solution.py:508
  129.8 1.7 %copy.22 = bf16[64,2048]{1,0:T(8,128)(2,1)} copy(bf16[64,2048]{1,0:T(8,128)(2,1)} %shard_map.100) | data formatting | bytes 524288
Async XLA Ops:
  0.0 7.6 %copy-start = (bf16[2048,704]{0,1:T(8,128)(2,1)S(1)}, bf16[2048,704]{0,1:T(8,128)(2,1)}, u32[]{:S(2)}) copy-start(bf16[2048,704]{0,1:T(8,128)(2,1)} %param.19) | copy-start | bytes 8650756

commit v2 on v1

--- a/solution.py
+++ b/solution.py
@@ -141,7 +141,8 @@
     attn_ref,
     gain_ref,
     residual_ref,
-    w_ref,
+    routes_ref,
+    logits_ref,
     o_hbm,
     ein_hbm,
     eout_hbm,
@@ -160,6 +161,7 @@
     rows_all,
     partial,
     core_in,
+    w_mine,
     w_all,
     w_cols,
     active,
@@ -213,6 +215,12 @@
     for peer in [(other, y) for other in others] + [y_peer]:
         pl.semaphore_signal(barrier, inc=1, device_id=peer, device_id_type=pl.DeviceIdType.MESH)
 
+    sigmoids = jax.nn.sigmoid(logits_ref[...])
+    weights = 2.446 * sigmoids / jnp.sum(sigmoids, axis=0, keepdims=True)
+    for e in range(16):
+        named = jnp.where(routes_ref[...] == e, weights, 0.0)
+        w_mine[e] = jnp.broadcast_to(jnp.sum(named, axis=0, keepdims=True), (8, 128))
+
     for i, (start, size) in enumerate(o_tiles):
         o_loads[i].wait()
         products[:, start : start + size] = jnp.dot(
@@ -231,12 +239,12 @@
     for q in range(PIECES):
         y_copy(q).start()
     w_copies = [
-        remote(w_ref.at[other], w_all.at[ep], w_send.at[i], w_recv.at[i], (other, y))
+        remote(w_mine.at[other], w_all.at[ep], w_send.at[i], w_recv.at[i], (other, y))
         for i, other in enumerate(others)
     ]
     for copy in w_copies:
         copy.start()
-    w_all[ep] = w_ref[ep]
+    w_all[ep] = w_mine[ep]
 
     def block(ref, q, index, cols):
         return ref.at[q, index["z"], index["x"], core, index["y"], :, cols]
@@ -321,17 +329,19 @@
         gather_core(q).wait_recv()
 
     def gate_up(rows, w_in, start, size):
-        gate = jnp.dot(rows, w_in[0, :, start : start + size], preferred_element_type=f32)
-        up = jnp.dot(rows, w_in[1, :, start : start + size], preferred_element_type=f32)
-        return jax.nn.silu(gate) * up
+        both = [
+            lax.dot_general(
+                rows, w_in[i, start : start + size, :], (((1,), (1,)), ((), ())),
+                preferred_element_type=f32,
+            )
+            for i in range(2)
+        ]
+        return jax.nn.silu(both[0]) * both[1]
 
     def down(act, w_out, start, size):
-        return lax.dot_general(
-            act, w_out[start : start + size, :], (((1,), (1,)), ((), ())),
-            preferred_element_type=f32,
-        )
-
-    hidden_tiles = tiles(ein.shape[2], HIDDEN_TILES)
+        return jnp.dot(act, w_out[:, start : start + size], preferred_element_type=f32)
+
+    hidden_tiles = tiles(ein.shape[1], HIDDEN_TILES)
     out_tiles = tiles(width, OUT_TILES)
 
     def expert_in_tile(i):
@@ -488,9 +498,11 @@
         copy.wait_send()
 
 
-def fused(attn, gain, residual, weights, o_weight, expert_in, expert_out, shared_in, shared_out):
+def fused(
+    attn, gain, residual, routes, logits, o_weight, expert_in, expert_out, shared_in, shared_out
+):
     rows, width = residual.shape
-    hidden_units = expert_in.shape[3]
+    hidden_units = expert_in.shape[2]
     bf16, f32 = jnp.bfloat16, jnp.float32
     boxes = []
     for _, size, order in TRACKS:
@@ -508,7 +520,7 @@
     return pl.pallas_call(
         fused_kernel,
         out_shape=jax.ShapeDtypeStruct((rows, width), bf16),
-        in_specs=[vmem] * 4 + [hbm] * 5,
+        in_specs=[vmem] * 5 + [hbm] * 5,
         out_specs=vmem,
         scratch_shapes=[
             pltpu.VMEM(o_weight.shape, bf16),
@@ -523,6 +535,7 @@
             pltpu.VMEM((PIECES, 4, 2, 2, 2, PIECE_ROWS, width), bf16),
             pltpu.VMEM((PIECES, 4, 2, 2, 2, PIECE_ROWS, width), bf16),
             pltpu.VMEM((PIECES, 4, 2, 2, PIECE_ROWS, width), bf16),
+            pltpu.VMEM((16, 8, 128), f32),
             pltpu.VMEM((16, 8, 128), f32),
             pltpu.VMEM((PIECES, 32 * PIECE_ROWS, 128), f32),
             pltpu.VMEM((32 * PIECE_ROWS, hidden_units), bf16),
@@ -546,7 +559,7 @@
         compiler_params=pltpu.CompilerParams(
             collective_id=0, has_side_effects=True, vmem_limit_bytes=60 * 1024 * 1024
         ),
-    )(attn, gain, residual, weights, o_weight, expert_in, expert_out, shared_in, shared_out)
+    )(attn, gain, residual, routes, logits, o_weight, expert_in, expert_out, shared_in, shared_out)
 
 
 def fused_shards(
@@ -561,21 +574,17 @@
     shared_in,
     shared_out,
 ):
-    experts = expert_in.shape[0] * lax.axis_size("ep")
-    weights = route_weights(route_logits)
-    chosen = routes[:, :, None] == jnp.arange(experts, dtype=jnp.int32)[None, None, :]
-    dense_weights = jnp.sum(jnp.where(chosen, weights[:, :, None], 0.0), axis=1)
-    out_weights = jnp.broadcast_to(dense_weights.T[:, None, :], (experts, 8, routes.shape[0]))
     return fused(
         attn,
         norm_gain[None, :],
         residual,
-        out_weights,
+        routes.T,
+        route_logits.T,
         o_weight,
-        expert_in,
-        expert_out,
-        shared_in,
-        shared_out,
+        jnp.swapaxes(expert_in, 2, 3),
+        jnp.swapaxes(expert_out, 1, 2),
+        jnp.swapaxes(shared_in, 1, 2),
+        shared_out.T,
     )
 
 

time: 132 us -> 105 us (0.80)
  local copies, waits for them, and re-layouts: 26.8 us -> 1.67 us
  other arithmetic: 2.28 us -> 0 us
    unnamed x7 -> x1, local copies, waits for them, and re-layouts: 26.2 us -> 1.67 us
    reduce_sum x2 -> x0, other arithmetic: 1.56 us -> none  [the longest x1 0.86 us: route_weights(): return 2.446 * sigmoids / jnp.sum(sigmoids, axis=-1, keepdims=True)]
where the time goes in v2:
time: 105 us
  Pallas kernels  103 us (98%)
  local copies, waits for them, and re-layouts  1.67 us (2%)
    pallas_call x1, Pallas kernels, fused(): pl.pallas_call(fused_kernel, out_shape=jax.ShapeDtypeStruct((rows, width)...  103 us

profile of v2, /device:TPU:0, one launch (start us, length us, event | category | flops | bytes accessed | tf_op | source)
XLA Modules:
  0.0 104.8 jit_solution(12618318052472240046)
XLA Ops:
  0.0 103.1 %shard_map.100 = bf16[64,2048]{1,0:T(8,128)(2,1)} custom-call(bf16[128,1024]{1,0:T(8,128)(2,1)} %attn_ref.1, f32[1,2048]{1,0:T(1,128)} %bitcast.11, bf16[64,2048]{1,0:T(8,128)(2,1)} %residual_ref.1, s32[6,128]{1,0:T(8,128)} %bitcast.12, f32[6,128]{1,0:T(8,128)} %bitcast.13, bf16[1024,2048]{1,0:T(8,128)(2,1)} %o_hbm.1, bf16[1,2,704,2048]{3,2,1,0:T(8,128)(2,1)} %bitcast.7, ...), custom_call_target="tpu_custom_call" | custom-call | tf_op jit(solution)/shard_map/pallas_call | solution.py:520
  103.2 1.7 %copy.12 = bf16[64,2048]{1,0:T(8,128)(2,1)} copy(bf16[64,2048]{1,0:T(8,128)(2,1)} %shard_map.100) | data formatting | bytes 524288
